TPU v7x, 32 devices: a whole 2x2x4 slice. The times are simulated.
32 devices in a mesh: replica: 4 (over z), expert: 4 (over y, core), fsdp: 2 (over x).
Axes of the slice: x: 2, y: 2, z: 4, core: 2. Of those that a mesh axis runs over, the one named last changes fastest.
Arguments:
- tokens: bfloat16 [2048, 4096], P(('replica', 'expert'), 'fsdp'), may hold values from -6 to 6
- expert_ids: int32 [2048, 2], P(('replica', 'expert')), may hold values from 0 to 3, all different within a row; in each aligned block of 128 rows (0 to 127, 128 to 255, ...) at most 80 rows name the same one
- router: float32 [4, 4096], P('expert'), may hold values from -5 to 5
- router_moment: float32 [4, 4096], P('expert'), may hold values from -3 to 3
- router_grads: float32 [4, 4, 4096], P('replica', 'expert'), may hold values from -3 to 3
- kv_weight: float32 [4096, 1024], P('expert', 'fsdp'), may hold values from -5 to 5
- kv_moment: float32 [4096, 1024], P('expert', 'fsdp'), may hold values from -3 to 3
- kv_grads: float32 [4, 4096, 1024], P('replica', 'expert', 'fsdp'), may hold values from -3 to 3
- w_gate: bfloat16 [4, 4096, 1024], P('expert', None, 'fsdp'), may hold values from -0.09375 to 0.09375
- w_up: bfloat16 [4, 4096, 1024], P('expert', None, 'fsdp'), may hold values from -0.09375 to 0.09375
- w_down: bfloat16 [4, 1024, 4096], P('expert', 'fsdp'), may hold values from -0.1875 to 0.1875
Outputs:
- mixture: bfloat16 [2048, 4096], P(('replica', 'expert'), 'fsdp')
- router_next: float32 [4, 4096], P('expert')
- router_moment_next: float32 [4, 4096], P('expert')
- kv_next: float32 [4096, 1024], P('expert', 'fsdp')
- kv_moment_next: float32 [4096, 1024], P('expert', 'fsdp')
Inputs may be any that keep to these rules, and one draw needn't show every extreme that they name: `expert_ids`: each row names 2 different experts. Within the rows of one replica and expert index (aligned blocks of 128 rows) no expert is named more than 80 times, a bound that some block reaches.
All inputs are finite; a program needn't handle non-finite values.
Results may differ from a plain program's by a relative error of at most 0.015.
Values may be sent and summed in bfloat16 or wider, within the bound.
A program may use at most 64 MiB of HBM per device.

v0:
```python
import math

import jax
import jax.numpy as jnp
from jax import lax
from jax.sharding import PartitionSpec as P

D = 4096


def advance(param, moment, mean):
    moment_next = 0.9 * moment + mean
    return (param - 0.7 * (mean + 0.9 * moment_next), moment_next)


def local(
    tokens,
    expert_ids,
    router,
    router_moment,
    router_grads,
    kv_weight,
    kv_moment,
    kv_grads,
    w_gate,
    w_up,
    w_down,
):
    replicas = lax.axis_size("replica")
    sums = (
        lax.psum(router_grads[0].astype(jnp.bfloat16), "replica").astype(jnp.float32),
        lax.psum(kv_grads[0].astype(jnp.bfloat16), "replica").astype(jnp.float32),
    )
    router_next, router_moment_next = advance(router, router_moment, sums[0] / replicas)
    kv_next, kv_moment_next = advance(kv_weight, kv_moment, sums[1] / replicas)
    experts_here = lax.axis_size("expert")
    local_rows = expert_ids.shape[0]
    choices_per = expert_ids.shape[1]
    capacity = 5 * local_rows * choices_per // (4 * experts_here)
    columns = jnp.arange(experts_here, dtype=jnp.int32)
    onehot = (expert_ids[:, :, None] == columns).astype(jnp.int32)
    named = jnp.sum(onehot, axis=1)
    before = jnp.cumsum(named, axis=0) - named
    position = jnp.sum(onehot * before[:, None, :], axis=2)
    slot_index = expert_ids * capacity + position
    slots_all = jnp.arange(experts_here * capacity, dtype=jnp.int32)
    assign = jnp.sum(
        (slot_index[None, :, :] == slots_all[:, None, None]).astype(jnp.float32), axis=2
    ).astype(jnp.bfloat16)
    router_row = router_next[0]
    gate_w = w_gate[0]
    up_w = w_up[0]
    down_w = w_down[0]
    outgoing = jnp.dot(assign, tokens, preferred_element_type=jnp.float32).astype(jnp.bfloat16)
    outgoing = outgoing.reshape(experts_here, capacity, tokens.shape[1])
    received = lax.all_to_all(outgoing, "expert", split_axis=0, concat_axis=0, tiled=True)
    sources = received.shape[0]
    count = received.shape[1]
    rows = received.reshape(sources * count, received.shape[2])
    piece = lax.all_gather(rows, "fsdp", axis=1, tiled=True)
    gate = jnp.dot(piece, gate_w, preferred_element_type=jnp.float32)
    up = jnp.dot(piece, up_w, preferred_element_type=jnp.float32)
    logit = jnp.dot(piece.astype(jnp.float32), router_row, precision=lax.Precision.HIGHEST)
    gate, up, logit = (gate, up, logit)
    hidden = (jax.nn.silu(gate) * up).astype(jnp.bfloat16)
    partial_value = jnp.dot(hidden, down_w, preferred_element_type=jnp.float32)
    summed = lax.psum_scatter(
        partial_value.astype(jnp.bfloat16), "fsdp", scatter_dimension=1, tiled=True
    ).astype(jnp.float32)
    score = jax.nn.sigmoid(logit / math.sqrt(D))
    weighted = (score[:, None] * summed).astype(jnp.bfloat16)
    back_weighted = lax.all_to_all(
        weighted.reshape(sources, count, weighted.shape[1]),
        "expert",
        split_axis=0,
        concat_axis=0,
        tiled=True,
    )
    back_score = lax.all_to_all(
        score.reshape(sources, count).astype(jnp.bfloat16),
        "expert",
        split_axis=0,
        concat_axis=0,
        tiled=True,
    ).astype(jnp.float32)
    gather_back = assign.T
    numer = jnp.dot(
        gather_back,
        back_weighted.reshape(experts_here * capacity, back_weighted.shape[2]),
        preferred_element_type=jnp.float32,
    )
    denom = jnp.dot(
        gather_back.astype(jnp.float32),
        back_score.reshape(experts_here * capacity),
        precision=lax.Precision.HIGHEST,
    )
    mixture = (numer / denom[:, None]).astype(jnp.bfloat16)
    return (mixture, router_next, router_moment_next, kv_next, kv_moment_next)


def solution(mesh):
    placed = (
        P(("replica", "expert"), "fsdp"),
        P(("replica", "expert"), None),
        P("expert", None),
        P("expert", None),
        P("replica", "expert", None),
        P("expert", "fsdp"),
        P("expert", "fsdp"),
        P("replica", "expert", "fsdp"),
        P("expert", None, "fsdp"),
        P("expert", None, "fsdp"),
        P("expert", "fsdp", None),
    )
    return jax.shard_map(
        local,
        mesh=mesh,
        in_specs=placed,
        out_specs=(
            P(("replica", "expert"), "fsdp"),
            P("expert", None),
            P("expert", None),
            P("expert", "fsdp"),
            P("expert", "fsdp"),
        ),
        check_vma=False,
    )
```

profile of v0, /device:TPU:0, one launch (start us, length us, event | category | flops | bytes accessed | tf_op | source)
XLA Modules:
  0.0 158.4 jit_solution(13727602931043479490)
XLA Ops:
  8.0 0.0 copy-start
  8.0 0.0 all-gather.2.cloned.1.call-start
  8.1 0.7 convert_reduce_fusion.1
  8.8 0.1 copy.23
  8.9 0.2 reduce_window_sum.11
  9.1 0.1 copy.25
  9.2 0.7 select_reduce_fusion
  9.9 0.7 multiply_add_fusion.2
  10.6 0.0 copy-done
  10.6 0.5 convolution_convert_fusion.1
  11.1 21.4 %all_to_all.16 = bf16[4,80,2048]{2,1,0:T(8,128)(2,1)} all-to-all(bf16[4,80,2048]{2,1,0:T(8,128)(2,1)S(1)} %bitcast.41), channel_id=1, replica_groups=mesh['replica'=4,'expert'=4,'fsdp'=2] {'expert'}, dimensions={0} | all-to-all | bytes 2621440 | tf_op jit(solution)/shard_map/all_to_all | solution.py:56
  32.5 0.0 all-gather.2.cloned.1.call-update
  32.6 0.0 reduce-scatter.2.cloned.1.call-start
  32.6 39.9 %all-gather.2.cloned.1.call-done = bf16[320,4096]{1,0:T(8,128)(2,1)} async-done(((bf16[320,2048]{1,0:T(8,128)(2,1)}), bf16[320,4096]{1,0:T(8,128)(2,1)}) %all-gather.2.cloned.1.call-update) | async-done | bytes 2621456 | tf_op jit(solution)/shard_map/all_gather | solution.py:60
  72.5 0.0 copy-start.1
  72.5 5.5 %fusion.3 = f32[320,512]{1,0:T(8,128)} fusion(bf16[320,4096]{1,0:T(8,128)(2,1)} %all-gather.2.cloned.1.call-done, bf16[1,4096,512]{2,1,0:T(8,128)(2,1)} %param.19), kind=kOutput, calls=%fused_computation.4 | convolution fusion | flops 1342177280 | bytes 7471104 | tf_op jit(solution)/shard_map/dot_general | solution.py:61
  77.9 0.0 copy-done.1
  77.9 8.2 %convolution_convert_fusion = bf16[320,4096]{1,0:T(8,128)(2,1)} fusion(bf16[1,512,4096]{2,1,0:T(8,128)(2,1)} %param.21, bf16[320,4096]{1,0:T(8,128)(2,1)S(1)} %copy-done.1, bf16[1,4096,512]{2,1,0:T(8,128)(2,1)} %param.20, f32[320,512]{1,0:T(8,128)} %fusion.3), kind=kOutput, calls=%fused_computation | convolution fusion | flops 2686648320 | bytes 14286848 | tf_op jit(solution)/shard_map/dot_general | solution.py:66
  86.1 0.0 reduce-scatter.2.cloned.1.call-update
  86.1 0.0 copy-start.6
  86.1 0.0 copy-start.4
  86.1 0.0 copy-start.5
  86.2 0.0 all-reduce.2.cloned.1.call-start
  86.2 2.7 %convert_bitcast_fusion = bf16[1024,512]{1,0:T(8,128)(2,1)} fusion(f32[1,1024,512]{2,1,0:T(8,128)} %param.18), kind=kLoop, calls=%fused_computation.17 | loop fusion | flops 524288 | bytes 3145728 | tf_op jit(solution)/shard_map/convert_element_type | solution.py:32
  88.9 0.0 all-reduce.2.cloned.1.call-update
  88.9 0.0 copy-done.6
  89.0 19.3 %psum.14 = bf16[1,4096]{1,0:T(2,128)(2,1)S(1)} all-reduce(bf16[1,4096]{1,0:T(2,128)(2,1)S(1)} %convert_bitcast_fusion.1), channel_id=1, replica_groups=mesh['replica'=4,'expert'=4,'fsdp'=2] {'replica'}, use_global_device_ids=true, to_apply=%region_4.5 | all-reduce | flops 4096 | bytes 16384 | tf_op jit(solution)/shard_map/psum | solution.py:31
  108.2 0.0 copy-done.4
  108.2 0.0 copy-done.5
  108.2 0.7 multiply_subtract_fusion.1
  108.9 0.0 copy-start.3
  108.9 2.2 %convolution_reduce_fusion = f32[320]{0:T(512)S(1)} fusion(bf16[320,4096]{1,0:T(8,128)(2,1)S(1)} %copy-done.1, f32[1,4096]{1,0:T(1,128)S(1)} %get-tuple-element.9), kind=kOutput, calls=%fused_computation.15 | convolution fusion | flops 15728640 | bytes 2639104 | tf_op jit(solution)/shard_map/dot_general | solution.py:63
  111.1 0.7 convert_element_type.91
  111.7 3.2 %all-to-all-start.2 = ((bf16[4,1,80]{2,1,0:T(2,128)(2,1)}), bf16[4,1,80]{2,1,0:T(2,128)(2,1)S(1)}, u32[]{:S(2)}, u32[]{:S(2)}) async-start(bf16[4,1,80]{2,1,0:T(2,128)(2,1)} %convert_element_type.91), calls=%async_computation.3 | async-start | bytes 4096 | tf_op jit(solution)/shard_map/all_to_all | solution.py:79
  115.0 9.0 %reduce-scatter.2.cloned.1.call-done = bf16[320,2048]{1,0:T(8,128)(2,1)} async-done(((bf16[320,4096]{1,0:T(8,128)(2,1)}), bf16[320,2048]{1,0:T(8,128)(2,1)}) %reduce-scatter.2.cloned.1.call-update) | async-done | bytes 1310736 | tf_op jit(solution)/shard_map/reduce_scatter | solution.py:67
  123.9 0.0 copy-start.2
  123.9 2.8 %multiply_convert_fusion = bf16[320,2048]{1,0:T(8,128)(2,1)} fusion(bf16[320,2048]{1,0:T(8,128)(2,1)} %reduce-scatter.2.cloned.1.call-done, f32[320]{0:T(512)S(1)} %get-tuple-element.8), kind=kLoop, calls=%fused_computation.7 | loop fusion | flops 1966080 | bytes 2622720 | tf_op jit(solution)/shard_map/convert_element_type | solution.py:71
  126.8 0.0 copy-done.3
  126.8 0.0 all-to-all-done.2
  126.8 4.3 %all-to-all-start.1 = ((bf16[4,80,2048]{2,1,0:T(8,128)(2,1)}), bf16[4,80,2048]{2,1,0:T(8,128)(2,1)}, u32[]{:S(2)}, u32[]{:S(2)}) async-start(bf16[4,80,2048]{2,1,0:T(8,128)(2,1)} %bitcast.8), calls=%async_computation.2 | async-start | bytes 2621440 | tf_op jit(solution)/shard_map/all_to_all | solution.py:72
  131.1 10.5 %all-reduce.2.cloned.1.call-done = bf16[1024,512]{1,0:T(8,128)(2,1)} async-done(((bf16[1024,512]{1,0:T(8,128)(2,1)}), bf16[1024,512]{1,0:T(8,128)(2,1)}) %all-reduce.2.cloned.1.call-update) | async-done | bytes 1048592 | tf_op jit(solution)/shard_map/psum | solution.py:32
  141.5 0.0 copy-done.2
  141.5 4.6 %multiply_subtract_fusion = (f32[1024,512]{1,0:T(8,128)}, f32[1024,512]{1,0:T(8,128)}) fusion(f32[1024,512]{1,0:T(8,128)S(1)} %copy-done.2, bf16[1024,512]{1,0:T(8,128)(2,1)} %all-reduce.2.cloned.1.call-done, f32[1024,512]{1,0:T(8,128)} %param.17), kind=kLoop, calls=%fused_computation.10 | loop fusion | flops 4194304 | bytes 9437184 | tf_op jit(solution)/shard_map/sub | solution.py:13
  146.2 0.1 reshape.74
  146.3 0.1 convolution_bitcast_fusion
  146.4 2.0 %all-to-all-done.1 = bf16[4,80,2048]{2,1,0:T(8,128)(2,1)} async-done(((bf16[4,80,2048]{2,1,0:T(8,128)(2,1)}), bf16[4,80,2048]{2,1,0:T(8,128)(2,1)}, u32[]{:S(2)}, u32[]{:S(2)}) %all-to-all-start.1) | async-done | bytes 1310752 | tf_op jit(solution)/shard_map/all_to_all | solution.py:72
  148.4 2.6 %fusion.5 = bf16[128,2048]{1,0:T(8,128)(2,1)} fusion(bf16[320,2048]{1,0:T(8,128)(2,1)} %bitcast.9, f32[128]{0:T(128)S(1)} %convolution_bitcast_fusion, bf16[320,128]{1,0:T(8,128)(2,1)S(1)} %convert_reduce_fusion), kind=kOutput, calls=%fused_computation.9 | convolution fusion | flops 168296448 | bytes 1917440 | tf_op jit(solution)/shard_map/dot_general | solution.py:87
  (5 shorter events, 0.1 us)
Async XLA Ops:
  8.0 2.6 %copy-start = (bf16[128,2048]{1,0:T(8,128)(2,1)S(1)}, bf16[128,2048]{1,0:T(8,128)(2,1)}, u32[]{:S(2)}) copy-start(bf16[128,2048]{1,0:T(8,128)(2,1)} %param.11) | copy-start | bytes 1572868
  8.0 64.4 %all-gather.2.cloned.1.call-start = ((), (), s32[]{:S(2)}) async-start(), calls=%async_computation.4 | async-start | bytes 3932160 | tf_op jit(solution)/shard_map/all_gather | solution.py:60
  32.6 91.4 %reduce-scatter.2.cloned.1.call-start = ((), (), s32[]{:S(2)}) async-start(), calls=%async_computation.5 | async-start | bytes 3932160 | tf_op jit(solution)/shard_map/reduce_scatter | solution.py:67
  72.5 5.5 %copy-start.1 = (bf16[320,4096]{1,0:T(8,128)(2,1)S(1)}, bf16[320,4096]{1,0:T(8,128)(2,1)}, u32[]{:S(2)}) copy-start(bf16[320,4096]{1,0:T(8,128)(2,1)} %all-gather.2.cloned.1.call-done) | copy-start | bytes 7864324
  86.1 2.8 %copy-start.6 = (f32[1,1,4096]{2,1,0:T(1,128)S(1)}, f32[1,1,4096]{2,1,0:T(1,128)}, u32[]{:S(2)}) copy-start(f32[1,1,4096]{2,1,0:T(1,128)} %param.15) | copy-start | bytes 49156
  86.1 22.1 %copy-start.4 = (f32[1,4096]{1,0:T(1,128)S(1)}, f32[1,4096]{1,0:T(1,128)}, u32[]{:S(2)}) copy-start(f32[1,4096]{1,0:T(1,128)} %param.13) | copy-start | bytes 49156
  86.1 22.1 %copy-start.5 = (f32[1,4096]{1,0:T(1,128)S(1)}, f32[1,4096]{1,0:T(1,128)}, u32[]{:S(2)}) copy-start(f32[1,4096]{1,0:T(1,128)} %param.14) | copy-start | bytes 49156
  86.2 55.4 %all-reduce.2.cloned.1.call-start = ((), (), s32[]{:S(2)}) async-start(), calls=%async_computation.6 | async-start | bytes 2097152 | tf_op jit(solution)/shard_map/psum | solution.py:32
  108.9 17.9 %copy-start.3 = (f32[1,4096]{1,0:T(1,128)}, f32[1,4096]{1,0:T(1,128)S(1)}, u32[]{:S(2)}) copy-start(f32[1,4096]{1,0:T(1,128)S(1)} %get-tuple-element.9) | copy-start | bytes 49156
  111.7 15.0 %all-to-all-start.2 = ((bf16[4,1,80]{2,1,0:T(2,128)(2,1)}), bf16[4,1,80]{2,1,0:T(2,128)(2,1)S(1)}, u32[]{:S(2)}, u32[]{:S(2)}) async-start(bf16[4,1,80]{2,1,0:T(2,128)(2,1)} %convert_element_type.91), calls=%async_computation.3 | async-start | bytes 4096 | tf_op jit(solution)/shard_map/all_to_all | solution.py:79
  123.9 17.6 %copy-start.2 = (f32[1024,512]{1,0:T(8,128)S(1)}, f32[1024,512]{1,0:T(8,128)}, u32[]{:S(2)}) copy-start(f32[1024,512]{1,0:T(8,128)} %param.16) | copy-start | bytes 6291460
  126.8 21.6 %all-to-all-start.1 = ((bf16[4,80,2048]{2,1,0:T(8,128)(2,1)}), bf16[4,80,2048]{2,1,0:T(8,128)(2,1)}, u32[]{:S(2)}, u32[]{:S(2)}) async-start(bf16[4,80,2048]{2,1,0:T(8,128)(2,1)} %bitcast.8), calls=%async_computation.2 | async-start | bytes 2621440 | tf_op jit(solution)/shard_map/all_to_all | solution.py:72
Sparse Core Ops, SparseCore 0:
  32.7 39.7 all-gather.1
  86.2 37.6 reduce-scatter.1
Sparse Core Ops, SparseCore 1:
  89.6 51.9 all-reduce.1
where the time goes:
time: 159 us; the launch traced here: 158 us
  waiting for transfers between devices  61.4 us (39%)
  blocking collectives  40.7 us (26%)
  matrix products  19 us (12%)
  between operations  15.6 us (10%)
  other arithmetic  13.2 us (8%)
  starting transfers between devices  7.66 us (5%)
    all_gather x1, waiting for transfers between devices, local(): piece = lax.all_gather(rows, 'fsdp', axis=1, tiled=True)  39.9 us
    all_to_all x1, blocking collectives, local(): lax.all_to_all(outgoing, 'expert', split_axis=0, concat_axis=0, tiled=True)  21.4 us
    psum x1, blocking collectives, local(): lax.psum(router_grads[0].astype(jnp.bfloat16), 'replica')  19.3 us
    psum x1, waiting for transfers between devices, local(): lax.psum(kv_grads[0].astype(jnp.bfloat16), 'replica').astype(jnp.float32)  10.5 us
    reduce_scatter x1, waiting for transfers between devices, local(): lax.psum_scatter(partial_value.astype(jnp.bfloat16), 'fsdp', scatter_dime...  8.99 us
    dot_general x1, matrix products, local(): partial_value = jnp.dot(hidden, down_w, preferred_element_type=jnp.float32)  8.15 us
    dot_general x1, matrix products, local(): gate = jnp.dot(piece, gate_w, preferred_element_type=jnp.float32)  5.48 us
    sub x2, other arithmetic, advance(): return (param - 0.7 * (mean + 0.9 * moment_next), moment_next)  5.27 us
  transfers between devices with their start and end apart: 5, of which 4 were waited for; matrix products, arithmetic and copies ran while one was open for 9% of the time, Pallas kernels for 0%

commit v1 on v0

--- a/solution.py
+++ b/solution.py
@@ -1,19 +1,24 @@
+import functools
 import math
 
 import jax
 import jax.numpy as jnp
 from jax import lax
+from jax.experimental import pallas as pl
+from jax.experimental.pallas import tpu as pltpu
 from jax.sharding import PartitionSpec as P
 
 D = 4096
-
+MESH = pl.DeviceIdType.MESH
+F32 = jnp.float32
+BF16 = jnp.bfloat16
 
 def advance(param, moment, mean):
     moment_next = 0.9 * moment + mean
     return (param - 0.7 * (mean + 0.9 * moment_next), moment_next)
 
 
-def local(
+def general(
     tokens,
     expert_ids,
     router,
@@ -98,6 +103,494 @@
     return (mixture, router_next, router_moment_next, kv_next, kv_moment_next)
 
 
+def tile_of(extent, want):
+    while extent % want:
+        want //= 2
+    return want
+
+
+def kernel(
+    capacity,
+    tokens,
+    ids,
+    router,
+    router_moment,
+    router_grads,
+    kv_weight,
+    kv_moment,
+    kv_grads,
+    w_gate,
+    w_up,
+    w_down,
+    mixture,
+    router_next,
+    router_moment_next,
+    kv_next,
+    kv_moment_next,
+    tok,
+    idbuf,
+    rbuf,
+    wg,
+    wu,
+    wd,
+    rows,
+    gacc,
+    uacc,
+    lacc,
+    hidden,
+    score,
+    dsrc,
+    dens,
+    outp,
+    sib,
+    xa,
+    yb,
+    ya2,
+    xb2,
+    mixed,
+    kg,
+    kw,
+    km,
+    kvb,
+    kr1,
+    kr2,
+    kfin,
+    ssem,
+    rsem,
+    lsem,
+    osem,
+):
+    z = lax.axis_index("replica")
+    e = lax.axis_index("expert")
+    x = lax.axis_index("fsdp")
+    half_e = lax.axis_size("expert") // 2
+    replicas = lax.axis_size("replica")
+    core = e % 2
+    e_sib = e + 1 - 2 * core
+    e_y = (e + half_e) % (2 * half_e)
+    e_diag = e_y + 1 - 2 * core
+    sibling = {"expert": e_sib}
+    xn = {"fsdp": 1 - x}
+    yn = {"expert": e_y}
+    diag = {"expert": e_diag}
+    z_one = {"replica": z + 1 - 2 * (z % 2)}
+    z_two = {"replica": (z + 2) % replicas}
+    n_tok, feat = tokens.shape
+    upper = n_tok // 2
+    hid = wg.shape[1]
+    kv_rows = kg.shape[0] // 4
+    used = []
+
+    def send(src, dst, number, device):
+        copy = pltpu.make_async_remote_copy(
+            src_ref=src,
+            dst_ref=dst,
+            send_sem=ssem.at[number],
+            recv_sem=rsem.at[number],
+            device_id=device,
+            device_id_type=MESH,
+        )
+        copy.start()
+        used.append(copy)
+
+    def arrive(dst, number, device):
+        pltpu.make_async_remote_copy(
+            src_ref=dst,
+            dst_ref=dst,
+            send_sem=ssem.at[number],
+            recv_sem=rsem.at[number],
+            device_id=device,
+            device_id_type=MESH,
+        ).wait_recv()
+
+    def load(src, dst, number):
+        copy = pltpu.make_async_copy(src, dst, lsem.at[number])
+        copy.start()
+        return copy
+
+    A = pl.ds(0, upper)
+    B = pl.ds(upper, upper)
+
+    get_grads = load(kv_grads.at[0], kg, 0)
+    get_own = load(tokens, tok.at[0, 1, 0], 1)
+    get_ids = load(ids, idbuf.at[0, 1], 2)
+    get_router = load(router_grads.at[0], rbuf.at[z], 3)
+
+    barrier = pltpu.get_barrier_semaphore()
+    peers = [sibling, xn, yn, diag] + [{"replica": (z + d) % replicas} for d in (1, 2, 3)]
+    for peer in peers:
+        pl.semaphore_signal(barrier, inc=1, device_id=peer, device_id_type=MESH)
+    pl.semaphore_wait(barrier, len(peers))
+
+    send(tokens.at[A], tok.at[0, 1, 1, A], 0, xn)
+    send(tokens.at[B], tok.at[1, 1, 0, B], 1, yn)
+    send(ids, idbuf.at[0, 0], 2, sibling)
+    send(ids, idbuf.at[1, 1], 3, yn)
+    send(ids, idbuf.at[1, 0], 4, diag)
+    for d in (1, 2, 3):
+        send(router_grads.at[0], rbuf.at[z], 4 + d, {"replica": (z + d) % replicas})
+    send(tokens.at[B], tok.at[0, 1, 1, B], 8, xn)
+    send(tokens.at[A], tok.at[1, 1, 0, A], 9, yn)
+    send(tokens, tok.at[0, 0, 0], 10, sibling)
+
+    low, high = z % 2, z // 2
+
+    def quarter(hr, qr):
+        index = ((low + hr) % 2) * 2 + (high + qr) % 2
+        return pl.multiple_of(index * kv_rows, kv_rows)
+
+    step = tile_of(kv_rows, 32)
+    get_grads.wait()
+    for hr in (1, 0):
+        for qr in (0, 1):
+            base = quarter(hr, qr)
+
+            @pl.loop(0, kv_rows // step)
+            def _(i):
+                at = pl.multiple_of(i * step, step)
+                kvb[hr, qr, pl.ds(at, step)] = kg[pl.ds(pl.multiple_of(base + at, step), step)].astype(BF16)
+
+        if hr == 1:
+            send(kvb.at[1], kr1, 11, z_one)
+
+    get_gate = load(w_gate.at[0], wg, 4)
+    get_up = load(w_up.at[0], wu, 5)
+    get_down = load(w_down.at[0], wd, 6)
+    get_kw = load(kv_weight, kw, 7)
+    get_km = load(kv_moment, km, 8)
+
+    arrive(tok.at[0, 1, 1, A], 0, xn)
+    send(tok.at[0, 1, 1, A], tok.at[1, 1, 1, A], 12, yn)
+    send(tok.at[0, 1, 1, A], tok.at[0, 0, 1, A], 13, sibling)
+    arrive(tok.at[1, 1, 0, B], 1, yn)
+    send(tok.at[1, 1, 0, B], tok.at[1, 1, 1, B], 14, xn)
+    send(tok.at[1, 1, 0, B], tok.at[1, 0, 0, B], 15, sibling)
+
+    get_router.wait()
+    for d in (1, 2, 3):
+        source = (z + replicas - d) % replicas
+        arrive(rbuf.at[source], 4 + d, {"replica": source})
+    total = rbuf[0]
+    for r in range(1, replicas):
+        total = total + rbuf[r]
+    router_new, moment_new = advance(router[...], router_moment[...], total / replicas)
+    router_next[...] = router_new
+    router_moment_next[...] = moment_new
+
+    get_ids.wait()
+    arrive(idbuf.at[0, 0], 2, sibling)
+    arrive(idbuf.at[1, 1], 3, yn)
+    arrive(idbuf.at[1, 0], 4, diag)
+    before = (
+        lax.broadcasted_iota(jnp.int32, (n_tok, n_tok), 0)
+        < lax.broadcasted_iota(jnp.int32, (n_tok, n_tok), 1)
+    ).astype(F32).astype(BF16)
+
+    def pick(g, q):
+        named = idbuf[g, q]
+        hit = jnp.where(named == e.astype(F32), 1.0, 0.0)
+        chosen = jnp.sum(hit, axis=0, keepdims=True)
+        wide = jnp.broadcast_to(chosen, (16, n_tok))
+        place = jnp.dot(wide.astype(BF16), before, preferred_element_type=F32)[0:1]
+        slots = lax.broadcasted_iota(jnp.int32, (capacity, n_tok), 0).astype(F32)
+        return jnp.where((slots == place) & (chosen > 0.5), 1.0, 0.0)
+
+    arrive(tok.at[0, 1, 1, B], 8, xn)
+    send(tok.at[0, 1, 1, B], tok.at[0, 0, 1, B], 16, sibling)
+    arrive(tok.at[1, 1, 0, A], 9, yn)
+    send(tok.at[1, 1, 0, A], tok.at[1, 0, 0, A], 17, sibling)
+
+    def fold(dst, one, two):
+        @pl.loop(0, one.shape[0] // step)
+        def _(i):
+            at = pl.ds(pl.multiple_of(i * step, step), step)
+            dst[at] = (one[at].astype(F32) + two[at].astype(F32)).astype(BF16)
+
+    arrive(kr1, 11, z_one)
+    fold(kvb.at[0, 1], kvb.at[0, 1], kr1.at[1])
+    send(kvb.at[0, 1], kr2, 18, z_two)
+    fold(kvb.at[0, 0], kvb.at[0, 0], kr1.at[0])
+
+    cols = tile_of(feat, 512)
+    per = feat // cols
+
+    def expert_rows(g):
+        picks = [pick(g, q) for q in (0, 1)]
+        lacc[...] = jnp.zeros_like(lacc)
+        gacc[...] = jnp.zeros_like(gacc)
+        uacc[...] = jnp.zeros_like(uacc)
+        narrow = [p.astype(BF16) for p in picks]
+        for xr in (0, 1):
+            @pl.loop(0, per)
+            def _(n):
+                here = pl.ds(pl.multiple_of(n * cols, cols), cols)
+                deep = pl.ds(pl.multiple_of(((x + xr) % 2) * feat + n * cols, cols), cols)
+                for q in (0, 1):
+                    rows[pl.ds(q * capacity, capacity)] = jnp.dot(
+                        narrow[q], tok[g, q, xr, :, here], preferred_element_type=F32
+                    ).astype(BF16)
+                block = rows[...]
+                gacc[...] += jnp.dot(block, wg[deep], preferred_element_type=F32)
+                uacc[...] += jnp.dot(block, wu[deep], preferred_element_type=F32)
+                prod = block.astype(F32) * router_next[:, deep]
+                part = prod[:, 0:128]
+                for j in range(1, cols // 128):
+                    part = part + prod[:, j * 128 : (j + 1) * 128]
+                lacc[...] += part
+
+        gate = gacc[...]
+        hidden[...] = (gate / (1.0 + jnp.exp(-gate)) * uacc[...]).astype(BF16)
+        logit = jnp.sum(lacc[...], axis=1, keepdims=True) / math.sqrt(2 * feat)
+        score[...] = jnp.broadcast_to(1.0 / (1.0 + jnp.exp(-logit)), score.shape)
+        for q in (0, 1):
+            spread = lax.dot_general(
+                picks[q],
+                score[pl.ds(q * capacity, capacity)],
+                (((0,), (0,)), ((), ())),
+                precision=lax.Precision.HIGHEST,
+                preferred_element_type=F32,
+            )
+            if (g, q) == (0, 1):
+                dens[0] = spread
+            else:
+                dsrc[g, q] = spread
+        if g == 0:
+            send(dsrc.at[0, 0], dens.at[1], 19, sibling)
+        else:
+            send(dsrc.at[1, 1], dens.at[2], 20, yn)
+            send(dsrc.at[1, 0], dens.at[3], 21, diag)
+        return narrow
+
+    def expert_out(g, narrow, xr):
+        @pl.loop(0, per)
+        def _(n):
+            here = pl.ds(pl.multiple_of(n * cols, cols), cols)
+            deep = pl.ds(pl.multiple_of(((x + xr) % 2) * feat + n * cols, cols), cols)
+            value = jnp.dot(hidden[...], wd[:, deep], preferred_element_type=F32)
+            for q in (0, 1):
+                own = slice(q * capacity, (q + 1) * capacity)
+                scaled = (value[own] * score[pl.ds(q * capacity, capacity), 0:1]).astype(BF16)
+                outp[g, q, xr, :, here] = lax.dot_general(
+                    narrow[q], scaled, (((0,), (0,)), ((), ())), preferred_element_type=F32
+                ).astype(BF16)
+
+    rstep = tile_of(upper, 16)
+
+    def add_rows(dst, one, two, lo, count):
+        @pl.loop(0, count // rstep)
+        def _(i):
+            at = pl.ds(pl.multiple_of(lo + i * rstep, rstep), rstep)
+            dst[at] = (one[at].astype(F32) + two[at].astype(F32)).astype(BF16)
+
+    def add_half(dst, lo, two):
+        @pl.loop(0, upper // rstep)
+        def _(i):
+            at = pl.ds(pl.multiple_of(lo + i * rstep, rstep), rstep)
+            there = pl.ds(pl.multiple_of(i * rstep, rstep), rstep)
+            dst[at] = (dst[at].astype(F32) + two[there].astype(F32)).astype(BF16)
+
+    get_own.wait()
+    arrive(tok.at[0, 0, 0], 10, sibling)
+    arrive(tok.at[0, 0, 1, A], 13, sibling)
+    arrive(tok.at[0, 0, 1, B], 16, sibling)
+    get_gate.wait()
+    get_up.wait()
+    narrow = expert_rows(0)
+    get_down.wait()
+
+    arrive(tok.at[1, 1, 1, A], 12, yn)
+    send(tok.at[1, 1, 1, A], tok.at[1, 0, 1, A], 22, sibling)
+    arrive(tok.at[1, 1, 1, B], 14, xn)
+    send(tok.at[1, 1, 1, B], tok.at[1, 0, 1, B], 23, sibling)
+
+    expert_out(0, narrow, 1)
+    send(outp.at[0, 0, 1], sib.at[0, 1], 24, sibling)
+    expert_out(0, narrow, 0)
+    send(outp.at[0, 0, 0], sib.at[0, 0], 25, sibling)
+
+    arrive(kr2, 18, z_two)
+    fold(kfin.at[0, 0], kvb.at[0, 0], kr2)
+    send(kfin.at[0, 0], kfin.at[0, 1], 26, z_two)
+
+    arrive(sib.at[0, 1], 24, sibling)
+    add_rows(outp.at[0, 1, 1], outp.at[0, 1, 1], sib.at[0, 1], 0, n_tok)
+    send(outp.at[0, 1, 1, A], xa.at[0], 27, xn)
+    arrive(tok.at[1, 0, 0, B], 15, sibling)
+    arrive(tok.at[1, 0, 0, A], 17, sibling)
+    arrive(tok.at[1, 0, 1, A], 22, sibling)
+    arrive(tok.at[1, 0, 1, B], 23, sibling)
+    narrow = expert_rows(1)
+    expert_out(1, narrow, 1)
+    send(outp.at[1, 0, 1], sib.at[1, 1], 28, sibling)
+    expert_out(1, narrow, 0)
+    send(outp.at[1, 0, 0], sib.at[1, 0], 29, sibling)
+    arrive(sib.at[1, 1], 28, sibling)
+    add_rows(outp.at[1, 1, 1], outp.at[1, 1, 1], sib.at[1, 1], 0, n_tok)
+    send(outp.at[1, 1, 1, A], xa.at[1], 30, xn)
+    send(outp.at[1, 1, 1, B], yb.at[1], 31, yn)
+    arrive(sib.at[1, 0], 29, sibling)
+    add_rows(outp.at[1, 1, 0], outp.at[1, 1, 0], sib.at[1, 0], 0, n_tok)
+    send(outp.at[1, 1, 0, B], yb.at[0], 32, yn)
+
+    arrive(kfin.at[0, 1], 26, z_two)
+    send(kfin.at[0], kfin.at[1], 33, z_one)
+
+    arrive(sib.at[0, 0], 25, sibling)
+    add_rows(outp.at[0, 1, 0], outp.at[0, 1, 0], sib.at[0, 0], 0, n_tok)
+
+    get_kw.wait()
+    get_km.wait()
+    outs = []
+
+    def finish(hr):
+        for qr in (0, 1):
+            base = quarter(hr, qr)
+
+            @pl.loop(0, kv_rows // step)
+            def _(i):
+                at = pl.multiple_of(i * step, step)
+                deep = pl.ds(pl.multiple_of(base + at, step), step)
+                mean = kfin[hr, qr, pl.ds(at, step)].astype(F32) / replicas
+                value, moment = advance(kw[deep], km[deep], mean)
+                kw[deep] = value
+                km[deep] = moment
+
+            whole = pl.ds(base, kv_rows)
+            for k, (src, dst) in enumerate(((kw, kv_next), (km, kv_moment_next))):
+                copy = pltpu.make_async_copy(src.at[whole], dst.at[whole], osem.at[hr * 4 + qr * 2 + k])
+                copy.start()
+                outs.append(copy)
+
+    arrive(xa.at[1], 30, xn)
+    add_half(outp.at[1, 1, 0], 0, xa.at[1])
+    send(outp.at[1, 1, 0, A], ya2, 34, yn)
+    arrive(yb.at[1], 31, yn)
+    add_half(outp.at[0, 1, 1], upper, yb.at[1])
+    send(outp.at[0, 1, 1, B], xb2, 35, xn)
+    finish(0)
+
+    arrive(xa.at[0], 27, xn)
+    arrive(yb.at[0], 32, yn)
+    arrive(dens.at[1], 19, sibling)
+    arrive(dens.at[2], 20, yn)
+    arrive(dens.at[3], 21, diag)
+    dens[0] = 1.0 / (dens[0] + dens[1] + dens[2] + dens[3])
+    arrive(kfin.at[1], 33, z_one)
+    finish(1)
+
+    def close(lo, first, second):
+        @pl.loop(0, upper // rstep)
+        def _(i):
+            at = pl.ds(pl.multiple_of(lo + i * rstep, rstep), rstep)
+            there = pl.ds(pl.multiple_of(i * rstep, rstep), rstep)
+            value = outp[0, 1, 0, at].astype(F32) + first[there].astype(F32)
+            value = value + second[there].astype(F32)
+            mixed[at] = (value * dens[0, at, 0:1]).astype(BF16)
+
+    arrive(ya2, 34, yn)
+    close(0, xa.at[0], ya2)
+    copy = pltpu.make_async_copy(mixed.at[A], mixture.at[A], osem.at[8])
+    copy.start()
+    outs.append(copy)
+    arrive(xb2, 35, xn)
+    close(upper, yb.at[0], xb2)
+    copy = pltpu.make_async_copy(mixed.at[B], mixture.at[B], osem.at[9])
+    copy.start()
+    outs.append(copy)
+    for copy in used:
+        copy.wait_send()
+    for copy in outs:
+        copy.wait()
+
+
+def fused(
+    tokens,
+    expert_ids,
+    router,
+    router_moment,
+    router_grads,
+    kv_weight,
+    kv_moment,
+    kv_grads,
+    w_gate,
+    w_up,
+    w_down,
+):
+    n_tok, feat = tokens.shape
+    choices = expert_ids.shape[1]
+    capacity = 5 * n_tok * choices // (4 * lax.axis_size("expert"))
+    hid = w_gate.shape[2]
+    kv_shape = kv_weight.shape
+    part = (kv_shape[0] // 4, kv_shape[1])
+    ids = jnp.pad(expert_ids.T.astype(F32), ((0, 8 - choices), (0, 0)), constant_values=-1.0)
+    hbm = pl.BlockSpec(memory_space=pl.ANY)
+    vmem = pl.BlockSpec(memory_space=pltpu.VMEM)
+    half = (n_tok // 2, feat)
+    cols = tile_of(feat, 512)
+    return pl.pallas_call(
+        functools.partial(kernel, capacity),
+        out_shape=(
+            jax.ShapeDtypeStruct(tokens.shape, BF16),
+            jax.ShapeDtypeStruct(router.shape, F32),
+            jax.ShapeDtypeStruct(router.shape, F32),
+            jax.ShapeDtypeStruct(kv_shape, F32),
+            jax.ShapeDtypeStruct(kv_shape, F32),
+        ),
+        in_specs=[hbm, hbm, vmem, vmem] + [hbm] * 7,
+        out_specs=(hbm, vmem, vmem, hbm, hbm),
+        scratch_shapes=[
+            pltpu.VMEM((2, 2, 2, n_tok, feat), BF16),
+            pltpu.VMEM((2, 2, 8, n_tok), F32),
+            pltpu.VMEM((lax.axis_size("replica"), 1, router.shape[1]), F32),
+            pltpu.VMEM(w_gate.shape[1:], BF16),
+            pltpu.VMEM(w_up.shape[1:], BF16),
+            pltpu.VMEM(w_down.shape[1:], BF16),
+            pltpu.VMEM((2 * capacity, cols), BF16),
+            pltpu.VMEM((2 * capacity, hid), F32),
+            pltpu.VMEM((2 * capacity, hid), F32),
+            pltpu.VMEM((2 * capacity, 128), F32),
+            pltpu.VMEM((2 * capacity, hid), BF16),
+            pltpu.VMEM((2 * capacity, 128), F32),
+            pltpu.VMEM((2, 2, n_tok, 128), F32),
+            pltpu.VMEM((4, n_tok, 128), F32),
+            pltpu.VMEM((2, 2, 2, n_tok, feat), BF16),
+            pltpu.VMEM((2, 2, n_tok, feat), BF16),
+            pltpu.VMEM((2,) + half, BF16),
+            pltpu.VMEM((2,) + half, BF16),
+            pltpu.VMEM(half, BF16),
+            pltpu.VMEM(half, BF16),
+            pltpu.VMEM((n_tok, feat), BF16),
+            pltpu.VMEM(kv_shape, F32),
+            pltpu.VMEM(kv_shape, F32),
+            pltpu.VMEM(kv_shape, F32),
+            pltpu.VMEM((2, 2) + part, BF16),
+            pltpu.VMEM((2,) + part, BF16),
+            pltpu.VMEM(part, BF16),
+            pltpu.VMEM((2, 2) + part, BF16),
+            pltpu.SemaphoreType.DMA((36,)),
+            pltpu.SemaphoreType.DMA((36,)),
+            pltpu.SemaphoreType.DMA((9,)),
+            pltpu.SemaphoreType.DMA((10,)),
+        ],
+        compiler_params=pltpu.CompilerParams(
+            collective_id=0, has_side_effects=True, vmem_limit_bytes=56 << 20
+        ),
+        name="step",
+    )(
+        tokens,
+        ids,
+        router,
+        router_moment,
+        router_grads,
+        kv_weight,
+        kv_moment,
+        kv_grads,
+        w_gate,
+        w_up,
+        w_down,
+    )
+
+
 def solution(mesh):
     placed = (
         P(("replica", "expert"), "fsdp"),
@@ -112,8 +605,11 @@
         P("expert", None, "fsdp"),
         P("expert", "fsdp", None),
     )
+    square = (
+        mesh.shape["replica"] == 4 and mesh.shape["expert"] == 4 and mesh.shape["fsdp"] == 2
+    )
     return jax.shard_map(
-        local,
+        fused if square else general,
         mesh=mesh,
         in_specs=placed,
         out_specs=(

time: 159 us -> 74.1 us (0.47)
  Pallas kernels: 0 us -> 62.6 us
  waiting for transfers between devices: 61.4 us -> 0 us
  blocking collectives: 40.7 us -> 0 us
  matrix products: 19 us -> 0 us
  between operations: 15.6 us -> 0.64 us
  other arithmetic: 13.2 us -> 0.68 us
  local copies, waits for them, and re-layouts: 0.98 us -> 9.68 us
  starting transfers between devices: 7.66 us -> 0 us
    pallas_call x0 -> x1, Pallas kernels: none -> 62.6 us  [fused(): pl.pallas_call(functools.partial(kernel, capacity), out_shape=(jax.ShapeD...]
    all_gather x1 -> x0, waiting for transfers between devices: 39.9 us -> none  [local(): piece = lax.all_gather(rows, 'fsdp', axis=1, tiled=True)]
    all_to_all x1 -> x0, blocking collectives: 21.4 us -> none  [local(): lax.all_to_all(outgoing, 'expert', split_axis=0, concat_axis=0, tiled=True)]
    psum x1 -> x0, blocking collectives: 19.3 us -> none  [local(): lax.psum(router_grads[0].astype(jnp.bfloat16), 'replica')]
    dot_general x6 -> x0, matrix products: 19 us -> none  [the longest x1 8.15 us: local(): partial_value = jnp.dot(hidden, down_w, preferred_element_type=jnp.float32)]
    psum x1 -> x0, waiting for transfers between devices: 10.5 us -> none  [local(): lax.psum(kv_grads[0].astype(jnp.bfloat16), 'replica').astype(jnp.float32)]
    unnamed x14 -> x7, local copies, waits for them, and re-layouts: 0.04 us -> 9.08 us
    reduce_scatter x1 -> x0, waiting for transfers between devices: 8.99 us -> none  [local(): lax.psum_scatter(partial_value.astype(jnp.bfloat16), 'fsdp', scatter_dime...]
  transfers between devices with their start and end apart: 5 -> 0, of which waited for: 4 -> 0; matrix products, arithmetic and copies ran while one was open for 9% -> 0% of each run, Pallas kernels for 0% -> 0%
where the time goes in v1:
time: 74.1 us; the launch traced here: 73.6 us
  Pallas kernels  62.6 us (84%)
  local copies, waits for them, and re-layouts  9.68 us (13%)
    pallas_call x1, Pallas kernels, fused(): pl.pallas_call(functools.partial(kernel, capacity), out_shape=(jax.ShapeD...  62.6 us
    unnamed x7, local copies, waits for them, and re-layouts  9.08 us

profile of v1, /device:TPU:0, one launch (start us, length us, event | category | flops | bytes accessed | tf_op | source)
XLA Modules:
  0.0 73.6 jit_solution(15263025271427067023)
XLA Ops:
  0.6 0.7 convert_bitcast_fusion
  1.3 0.6 pad.4.ids
  1.9 62.6 %step.1 = (bf16[128,2048]{1,0:T(8,128)(2,1)}, f32[1,4096]{1,0:T(1,128)}, f32[1,4096]{1,0:T(1,128)}, f32[1024,512]{1,0:T(8,128)}, f32[1024,512]{1,0:T(8,128)}) custom-call(bf16[128,2048]{1,0:T(8,128)(2,1)} %tokens.1, f32[8,128]{1,0:T(8,128)} %pad.4.ids, f32[1,4096]{1,0:T(1,128)} %router.1, f32[1,4096]{1,0:T(1,128)} %router_moment.1, ...), custom_call_target="tpu_custom_call" | custom-call | tf_op jit(solution)/shard_map/step/pallas_call | solution.py:530
  64.5 1.9 %copy.21 = bf16[128,2048]{1,0:T(8,128)(2,1)} copy(bf16[128,2048]{1,0:T(8,128)(2,1)} %get-tuple-element.10) | data formatting | bytes 1048576
  66.4 1.3 %copy.22 = f32[1,4096]{1,0:T(1,128)} copy(f32[1,4096]{1,0:T(1,128)} %get-tuple-element.11) | data formatting | bytes 32768
  67.7 1.3 %copy.23 = f32[1,4096]{1,0:T(1,128)} copy(f32[1,4096]{1,0:T(1,128)} %get-tuple-element.12) | data formatting | bytes 32768
  69.0 0.0 copy-start
  69.0 3.2 %copy.24 = f32[1024,512]{1,0:T(8,128)} copy(f32[1024,512]{1,0:T(8,128)} %get-tuple-element.13) | data formatting | bytes 4194304
  72.3 0.0 copy-done
  72.3 1.3 %copy.25 = f32[1024,512]{1,0:T(8,128)} copy(f32[1024,512]{1,0:T(8,128)S(1)} %copy-done) | data formatting | bytes 4194304
Async XLA Ops:
  69.0 3.2 %copy-start = (f32[1024,512]{1,0:T(8,128)S(1)}, f32[1024,512]{1,0:T(8,128)}, u32[]{:S(2)}) copy-start(f32[1024,512]{1,0:T(8,128)} %get-tuple-element.14) | copy-start | bytes 6291460

commit v2 on v1

--- a/solution.py
+++ b/solution.py
@@ -122,11 +122,11 @@
     w_gate,
     w_up,
     w_down,
-    mixture,
+    mixed,
     router_next,
     router_moment_next,
-    kv_next,
-    kv_moment_next,
+    kw,
+    km,
     tok,
     idbuf,
     rbuf,
@@ -147,18 +147,13 @@
     yb,
     ya2,
     xb2,
-    mixed,
     kg,
-    kw,
-    km,
     kvb,
-    kr1,
-    kr2,
+    kr,
     kfin,
     ssem,
     rsem,
     lsem,
-    osem,
 ):
     z = lax.axis_index("replica")
     e = lax.axis_index("expert")
@@ -173,12 +168,11 @@
     xn = {"fsdp": 1 - x}
     yn = {"expert": e_y}
     diag = {"expert": e_diag}
-    z_one = {"replica": z + 1 - 2 * (z % 2)}
-    z_two = {"replica": (z + 2) % replicas}
+    z_ids = ((z + 2) % replicas, replicas - 1 - z, z + 1 - 2 * (z % 2))
+    z_to = [{"replica": other} for other in z_ids]
     n_tok, feat = tokens.shape
     upper = n_tok // 2
     hid = wg.shape[1]
-    kv_rows = kg.shape[0] // 4
     used = []
 
     def send(src, dst, number, device):
@@ -211,10 +205,19 @@
     A = pl.ds(0, upper)
     B = pl.ds(upper, upper)
 
-    get_grads = load(kv_grads.at[0], kg, 0)
+    kv_rows = kg.shape[1]
+    get_grads = [
+        load(kv_grads.at[0, pl.ds(pl.multiple_of(other * kv_rows, kv_rows), kv_rows)], kg.at[k], (0, 2, 9, 10)[k])
+        for k, other in enumerate(z_ids + (z,))
+    ]
     get_own = load(tokens, tok.at[0, 1, 0], 1)
-    get_ids = load(ids, idbuf.at[0, 1], 2)
     get_router = load(router_grads.at[0], rbuf.at[z], 3)
+
+    named = jnp.full((n_tok, 128), -1.0, F32)
+    lane = lax.broadcasted_iota(jnp.int32, (n_tok, 128), 1)
+    for k in range(ids.shape[1]):
+        named = jnp.where(lane == k, ids[:, k : k + 1].astype(F32), named)
+    idbuf[0, 1] = named.T[0:8]
 
     barrier = pltpu.get_barrier_semaphore()
     peers = [sibling, xn, yn, diag] + [{"replica": (z + d) % replicas} for d in (1, 2, 3)]
@@ -224,34 +227,28 @@
 
     send(tokens.at[A], tok.at[0, 1, 1, A], 0, xn)
     send(tokens.at[B], tok.at[1, 1, 0, B], 1, yn)
-    send(ids, idbuf.at[0, 0], 2, sibling)
-    send(ids, idbuf.at[1, 1], 3, yn)
-    send(ids, idbuf.at[1, 0], 4, diag)
+    mine = idbuf.at[0, 1]
+    send(mine, idbuf.at[0, 0], 2, sibling)
+    send(mine, idbuf.at[1, 1], 3, yn)
+    send(mine, idbuf.at[1, 0], 4, diag)
     for d in (1, 2, 3):
         send(router_grads.at[0], rbuf.at[z], 4 + d, {"replica": (z + d) % replicas})
     send(tokens.at[B], tok.at[0, 1, 1, B], 8, xn)
     send(tokens.at[A], tok.at[1, 1, 0, A], 9, yn)
     send(tokens, tok.at[0, 0, 0], 10, sibling)
 
-    low, high = z % 2, z // 2
-
-    def quarter(hr, qr):
-        index = ((low + hr) % 2) * 2 + (high + qr) % 2
+    step = tile_of(kv_rows, 128)
+
+    def quarter(index):
         return pl.multiple_of(index * kv_rows, kv_rows)
 
-    step = tile_of(kv_rows, 32)
-    get_grads.wait()
-    for hr in (1, 0):
-        for qr in (0, 1):
-            base = quarter(hr, qr)
-
-            @pl.loop(0, kv_rows // step)
-            def _(i):
-                at = pl.multiple_of(i * step, step)
-                kvb[hr, qr, pl.ds(at, step)] = kg[pl.ds(pl.multiple_of(base + at, step), step)].astype(BF16)
-
-        if hr == 1:
-            send(kvb.at[1], kr1, 11, z_one)
+    for k, other in enumerate(z_ids + (z,)):
+        get_grads[k].wait()
+        for i in range(kv_rows // step):
+            at = pl.ds(i * step, step)
+            kvb[k, at] = kg[k, at].astype(BF16)
+        if k < 3:
+            send(kvb.at[k], kr.at[k], 11 + 7 * min(k, 1) + 8 * (k == 2), z_to[k])
 
     get_gate = load(w_gate.at[0], wg, 4)
     get_up = load(w_up.at[0], wu, 5)
@@ -259,12 +256,19 @@
     get_kw = load(kv_weight, kw, 7)
     get_km = load(kv_moment, km, 8)
 
-    arrive(tok.at[0, 1, 1, A], 0, xn)
-    send(tok.at[0, 1, 1, A], tok.at[1, 1, 1, A], 12, yn)
-    send(tok.at[0, 1, 1, A], tok.at[0, 0, 1, A], 13, sibling)
-    arrive(tok.at[1, 1, 0, B], 1, yn)
-    send(tok.at[1, 1, 0, B], tok.at[1, 1, 1, B], 14, xn)
-    send(tok.at[1, 1, 0, B], tok.at[1, 0, 0, B], 15, sibling)
+    def relay_first():
+        arrive(tok.at[0, 1, 1, A], 0, xn)
+        send(tok.at[0, 1, 1, A], tok.at[1, 1, 1, A], 12, yn)
+        send(tok.at[0, 1, 1, A], tok.at[0, 0, 1, A], 13, sibling)
+        arrive(tok.at[1, 1, 0, B], 1, yn)
+        send(tok.at[1, 1, 0, B], tok.at[1, 1, 1, B], 14, xn)
+        send(tok.at[1, 1, 0, B], tok.at[1, 0, 0, B], 15, sibling)
+
+    def relay_second():
+        arrive(tok.at[0, 1, 1, B], 8, xn)
+        send(tok.at[0, 1, 1, B], tok.at[0, 0, 1, B], 16, sibling)
+        arrive(tok.at[1, 1, 0, A], 9, yn)
+        send(tok.at[1, 1, 0, A], tok.at[1, 0, 0, A], 17, sibling)
 
     get_router.wait()
     for d in (1, 2, 3):
@@ -277,7 +281,6 @@
     router_next[...] = router_new
     router_moment_next[...] = moment_new
 
-    get_ids.wait()
     arrive(idbuf.at[0, 0], 2, sibling)
     arrive(idbuf.at[1, 1], 3, yn)
     arrive(idbuf.at[1, 0], 4, diag)
@@ -295,57 +298,56 @@
         slots = lax.broadcasted_iota(jnp.int32, (capacity, n_tok), 0).astype(F32)
         return jnp.where((slots == place) & (chosen > 0.5), 1.0, 0.0)
 
-    arrive(tok.at[0, 1, 1, B], 8, xn)
-    send(tok.at[0, 1, 1, B], tok.at[0, 0, 1, B], 16, sibling)
-    arrive(tok.at[1, 1, 0, A], 9, yn)
-    send(tok.at[1, 1, 0, A], tok.at[1, 0, 0, A], 17, sibling)
-
-    def fold(dst, one, two):
-        @pl.loop(0, one.shape[0] // step)
-        def _(i):
-            at = pl.ds(pl.multiple_of(i * step, step), step)
-            dst[at] = (one[at].astype(F32) + two[at].astype(F32)).astype(BF16)
-
-    arrive(kr1, 11, z_one)
-    fold(kvb.at[0, 1], kvb.at[0, 1], kr1.at[1])
-    send(kvb.at[0, 1], kr2, 18, z_two)
-    fold(kvb.at[0, 0], kvb.at[0, 0], kr1.at[0])
+    def sum_quarter():
+        for k in range(3):
+            arrive(kr.at[k], (11, 18, 26)[k], z_to[k])
+        for i in range(kv_rows // step):
+            at = pl.ds(i * step, step)
+            near = kvb[3, at].astype(F32) + kr[2, at].astype(F32)
+            far = kr[0, at].astype(F32) + kr[1, at].astype(F32)
+            kfin[3, at] = (near + far).astype(BF16)
+        for k in range(3):
+            send(kfin.at[3], kfin.at[k], (33, 36, 37)[k], z_to[k])
 
     cols = tile_of(feat, 512)
     per = feat // cols
 
-    def expert_rows(g):
-        picks = [pick(g, q) for q in (0, 1)]
-        lacc[...] = jnp.zeros_like(lacc)
-        gacc[...] = jnp.zeros_like(gacc)
-        uacc[...] = jnp.zeros_like(uacc)
-        narrow = [p.astype(BF16) for p in picks]
-        for xr in (0, 1):
-            @pl.loop(0, per)
-            def _(n):
-                here = pl.ds(pl.multiple_of(n * cols, cols), cols)
-                deep = pl.ds(pl.multiple_of(((x + xr) % 2) * feat + n * cols, cols), cols)
-                for q in (0, 1):
-                    rows[pl.ds(q * capacity, capacity)] = jnp.dot(
-                        narrow[q], tok[g, q, xr, :, here], preferred_element_type=F32
-                    ).astype(BF16)
-                block = rows[...]
-                gacc[...] += jnp.dot(block, wg[deep], preferred_element_type=F32)
-                uacc[...] += jnp.dot(block, wu[deep], preferred_element_type=F32)
-                prod = block.astype(F32) * router_next[:, deep]
-                part = prod[:, 0:128]
-                for j in range(1, cols // 128):
-                    part = part + prod[:, j * 128 : (j + 1) * 128]
-                lacc[...] += part
-
-        gate = gacc[...]
-        hidden[...] = (gate / (1.0 + jnp.exp(-gate)) * uacc[...]).astype(BF16)
-        logit = jnp.sum(lacc[...], axis=1, keepdims=True) / math.sqrt(2 * feat)
-        score[...] = jnp.broadcast_to(1.0 / (1.0 + jnp.exp(-logit)), score.shape)
+    picks, narrow = {}, {}
+
+    def expert_rows(g, xr):
+        if xr == 0:
+            picks[g] = [pick(g, q) for q in (0, 1)]
+            narrow[g] = [p.astype(BF16) for p in picks[g]]
+            lacc[g] = jnp.zeros(lacc.shape[1:], F32)
+            gacc[g] = jnp.zeros(gacc.shape[1:], F32)
+            uacc[g] = jnp.zeros(uacc.shape[1:], F32)
+
+        @pl.loop(0, per)
+        def _(n):
+            here = pl.ds(pl.multiple_of(n * cols, cols), cols)
+            deep = pl.ds(pl.multiple_of(((x + xr) % 2) * feat + n * cols, cols), cols)
+            for q in (0, 1):
+                rows[pl.ds(q * capacity, capacity)] = jnp.dot(
+                    narrow[g][q], tok[g, q, xr, :, here], preferred_element_type=F32
+                ).astype(BF16)
+            block = rows[...]
+            gacc[g] += jnp.dot(block, wg[deep], preferred_element_type=F32)
+            uacc[g] += jnp.dot(block, wu[deep], preferred_element_type=F32)
+            prod = block.astype(F32) * router_next[:, deep]
+            part = prod[:, 0:128]
+            for j in range(1, cols // 128):
+                part = part + prod[:, j * 128 : (j + 1) * 128]
+            lacc[g] += part
+
+    def expert_hidden(g):
+        gate = gacc[g]
+        hidden[...] = (gate / (1.0 + jnp.exp(-gate)) * uacc[g]).astype(BF16)
+        logit = jnp.sum(lacc[g], axis=1, keepdims=True) / math.sqrt(2 * feat)
+        score[g] = jnp.broadcast_to(1.0 / (1.0 + jnp.exp(-logit)), score.shape[1:])
         for q in (0, 1):
             spread = lax.dot_general(
-                picks[q],
-                score[pl.ds(q * capacity, capacity)],
+                picks[g][q],
+                score[g, pl.ds(q * capacity, capacity)],
                 (((0,), (0,)), ((), ())),
                 precision=lax.Precision.HIGHEST,
                 preferred_element_type=F32,
@@ -359,9 +361,8 @@
         else:
             send(dsrc.at[1, 1], dens.at[2], 20, yn)
             send(dsrc.at[1, 0], dens.at[3], 21, diag)
-        return narrow
-
-    def expert_out(g, narrow, xr):
+
+    def expert_out(g, xr):
         @pl.loop(0, per)
         def _(n):
             here = pl.ds(pl.multiple_of(n * cols, cols), cols)
@@ -369,60 +370,62 @@
             value = jnp.dot(hidden[...], wd[:, deep], preferred_element_type=F32)
             for q in (0, 1):
                 own = slice(q * capacity, (q + 1) * capacity)
-                scaled = (value[own] * score[pl.ds(q * capacity, capacity), 0:1]).astype(BF16)
+                scaled = (value[own] * score[g, pl.ds(q * capacity, capacity), 0:1]).astype(BF16)
                 outp[g, q, xr, :, here] = lax.dot_general(
-                    narrow[q], scaled, (((0,), (0,)), ((), ())), preferred_element_type=F32
+                    narrow[g][q], scaled, (((0,), (0,)), ((), ())), preferred_element_type=F32
                 ).astype(BF16)
 
-    rstep = tile_of(upper, 16)
+    rstep = tile_of(upper, 32)
 
     def add_rows(dst, one, two, lo, count):
         @pl.loop(0, count // rstep)
         def _(i):
             at = pl.ds(pl.multiple_of(lo + i * rstep, rstep), rstep)
-            dst[at] = (one[at].astype(F32) + two[at].astype(F32)).astype(BF16)
+            dst[at] = one[at] + two[at]
 
     def add_half(dst, lo, two):
         @pl.loop(0, upper // rstep)
         def _(i):
             at = pl.ds(pl.multiple_of(lo + i * rstep, rstep), rstep)
             there = pl.ds(pl.multiple_of(i * rstep, rstep), rstep)
-            dst[at] = (dst[at].astype(F32) + two[there].astype(F32)).astype(BF16)
-
+            dst[at] = dst[at] + two[there]
+
+    def diagonals():
+        arrive(tok.at[1, 1, 1, A], 12, yn)
+        send(tok.at[1, 1, 1, A], tok.at[1, 0, 1, A], 22, sibling)
+        arrive(tok.at[1, 1, 1, B], 14, xn)
+        send(tok.at[1, 1, 1, B], tok.at[1, 0, 1, B], 23, sibling)
+
+    get_gate.wait()
+    get_up.wait()
     get_own.wait()
     arrive(tok.at[0, 0, 0], 10, sibling)
+    expert_rows(0, 0)
+    relay_first()
+    relay_second()
     arrive(tok.at[0, 0, 1, A], 13, sibling)
     arrive(tok.at[0, 0, 1, B], 16, sibling)
-    get_gate.wait()
-    get_up.wait()
-    narrow = expert_rows(0)
+    expert_rows(0, 1)
+    expert_hidden(0)
     get_down.wait()
-
-    arrive(tok.at[1, 1, 1, A], 12, yn)
-    send(tok.at[1, 1, 1, A], tok.at[1, 0, 1, A], 22, sibling)
-    arrive(tok.at[1, 1, 1, B], 14, xn)
-    send(tok.at[1, 1, 1, B], tok.at[1, 0, 1, B], 23, sibling)
-
-    expert_out(0, narrow, 1)
+    expert_out(0, 1)
     send(outp.at[0, 0, 1], sib.at[0, 1], 24, sibling)
-    expert_out(0, narrow, 0)
-    send(outp.at[0, 0, 0], sib.at[0, 0], 25, sibling)
-
-    arrive(kr2, 18, z_two)
-    fold(kfin.at[0, 0], kvb.at[0, 0], kr2)
-    send(kfin.at[0, 0], kfin.at[0, 1], 26, z_two)
-
+    arrive(tok.at[1, 0, 0, B], 15, sibling)
+    arrive(tok.at[1, 0, 0, A], 17, sibling)
+    expert_rows(1, 0)
+    diagonals()
     arrive(sib.at[0, 1], 24, sibling)
     add_rows(outp.at[0, 1, 1], outp.at[0, 1, 1], sib.at[0, 1], 0, n_tok)
     send(outp.at[0, 1, 1, A], xa.at[0], 27, xn)
-    arrive(tok.at[1, 0, 0, B], 15, sibling)
-    arrive(tok.at[1, 0, 0, A], 17, sibling)
     arrive(tok.at[1, 0, 1, A], 22, sibling)
     arrive(tok.at[1, 0, 1, B], 23, sibling)
-    narrow = expert_rows(1)
-    expert_out(1, narrow, 1)
+    expert_rows(1, 1)
+    expert_out(0, 0)
+    send(outp.at[0, 0, 0], sib.at[0, 0], 25, sibling)
+    expert_hidden(1)
+    expert_out(1, 1)
     send(outp.at[1, 0, 1], sib.at[1, 1], 28, sibling)
-    expert_out(1, narrow, 0)
+    expert_out(1, 0)
     send(outp.at[1, 0, 0], sib.at[1, 0], 29, sibling)
     arrive(sib.at[1, 1], 28, sibling)
     add_rows(outp.at[1, 1, 1], outp.at[1, 1, 1], sib.at[1, 1], 0, n_tok)
@@ -432,34 +435,22 @@
     add_rows(outp.at[1, 1, 0], outp.at[1, 1, 0], sib.at[1, 0], 0, n_tok)
     send(outp.at[1, 1, 0, B], yb.at[0], 32, yn)
 
-    arrive(kfin.at[0, 1], 26, z_two)
-    send(kfin.at[0], kfin.at[1], 33, z_one)
+    sum_quarter()
 
     arrive(sib.at[0, 0], 25, sibling)
     add_rows(outp.at[0, 1, 0], outp.at[0, 1, 0], sib.at[0, 0], 0, n_tok)
 
     get_kw.wait()
     get_km.wait()
-    outs = []
-
-    def finish(hr):
-        for qr in (0, 1):
-            base = quarter(hr, qr)
-
-            @pl.loop(0, kv_rows // step)
-            def _(i):
-                at = pl.multiple_of(i * step, step)
-                deep = pl.ds(pl.multiple_of(base + at, step), step)
-                mean = kfin[hr, qr, pl.ds(at, step)].astype(F32) / replicas
-                value, moment = advance(kw[deep], km[deep], mean)
-                kw[deep] = value
-                km[deep] = moment
-
-            whole = pl.ds(base, kv_rows)
-            for k, (src, dst) in enumerate(((kw, kv_next), (km, kv_moment_next))):
-                copy = pltpu.make_async_copy(src.at[whole], dst.at[whole], osem.at[hr * 4 + qr * 2 + k])
-                copy.start()
-                outs.append(copy)
+
+    def finish(k):
+        base = quarter((z_ids + (z,))[k])
+        for i in range(kv_rows // step):
+            deep = pl.ds(pl.multiple_of(base + i * step, step), step)
+            mean = kfin[k, pl.ds(i * step, step)].astype(F32) / replicas
+            value, moment = advance(kw[deep], km[deep], mean)
+            kw[deep] = value
+            km[deep] = moment
 
     arrive(xa.at[1], 30, xn)
     add_half(outp.at[1, 1, 0], 0, xa.at[1])
@@ -467,7 +458,7 @@
     arrive(yb.at[1], 31, yn)
     add_half(outp.at[0, 1, 1], upper, yb.at[1])
     send(outp.at[0, 1, 1, B], xb2, 35, xn)
-    finish(0)
+    finish(3)
 
     arrive(xa.at[0], 27, xn)
     arrive(yb.at[0], 32, yn)
@@ -475,8 +466,6 @@
     arrive(dens.at[2], 20, yn)
     arrive(dens.at[3], 21, diag)
     dens[0] = 1.0 / (dens[0] + dens[1] + dens[2] + dens[3])
-    arrive(kfin.at[1], 33, z_one)
-    finish(1)
 
     def close(lo, first, second):
         @pl.loop(0, upper // rstep)
@@ -489,18 +478,13 @@
 
     arrive(ya2, 34, yn)
     close(0, xa.at[0], ya2)
-    copy = pltpu.make_async_copy(mixed.at[A], mixture.at[A], osem.at[8])
-    copy.start()
-    outs.append(copy)
     arrive(xb2, 35, xn)
     close(upper, yb.at[0], xb2)
-    copy = pltpu.make_async_copy(mixed.at[B], mixture.at[B], osem.at[9])
-    copy.start()
-    outs.append(copy)
+    for k in (2, 0, 1):
+        arrive(kfin.at[k], (33, 36, 37)[k], z_to[k])
+        finish(k)
     for copy in used:
         copy.wait_send()
-    for copy in outs:
-        copy.wait()
 
 
 def fused(
@@ -522,22 +506,22 @@
     hid = w_gate.shape[2]
     kv_shape = kv_weight.shape
     part = (kv_shape[0] // 4, kv_shape[1])
-    ids = jnp.pad(expert_ids.T.astype(F32), ((0, 8 - choices), (0, 0)), constant_values=-1.0)
-    hbm = pl.BlockSpec(memory_space=pl.ANY)
+    hbm = pl.BlockSpec(memory_space=pltpu.HBM)
     vmem = pl.BlockSpec(memory_space=pltpu.VMEM)
     half = (n_tok // 2, feat)
     cols = tile_of(feat, 512)
-    return pl.pallas_call(
+    outs = (
+        jax.ShapeDtypeStruct(tokens.shape, BF16),
+        jax.ShapeDtypeStruct(router.shape, F32),
+        jax.ShapeDtypeStruct(router.shape, F32),
+        jax.ShapeDtypeStruct(kv_shape, F32),
+        jax.ShapeDtypeStruct(kv_shape, F32),
+    )
+    held = pl.pallas_call(
         functools.partial(kernel, capacity),
-        out_shape=(
-            jax.ShapeDtypeStruct(tokens.shape, BF16),
-            jax.ShapeDtypeStruct(router.shape, F32),
-            jax.ShapeDtypeStruct(router.shape, F32),
-            jax.ShapeDtypeStruct(kv_shape, F32),
-            jax.ShapeDtypeStruct(kv_shape, F32),
-        ),
-        in_specs=[hbm, hbm, vmem, vmem] + [hbm] * 7,
-        out_specs=(hbm, vmem, vmem, hbm, hbm),
+        out_shape=tuple(pltpu.VMEM(o.shape, o.dtype) for o in outs),
+        in_specs=[hbm, vmem, vmem, vmem] + [hbm] * 7,
+        out_specs=(vmem,) * 5,
         scratch_shapes=[
             pltpu.VMEM((2, 2, 2, n_tok, feat), BF16),
             pltpu.VMEM((2, 2, 8, n_tok), F32),
@@ -546,11 +530,11 @@
             pltpu.VMEM(w_up.shape[1:], BF16),
             pltpu.VMEM(w_down.shape[1:], BF16),
             pltpu.VMEM((2 * capacity, cols), BF16),
-            pltpu.VMEM((2 * capacity, hid), F32),
-            pltpu.VMEM((2 * capacity, hid), F32),
-            pltpu.VMEM((2 * capacity, 128), F32),
+            pltpu.VMEM((2, 2 * capacity, hid), F32),
+            pltpu.VMEM((2, 2 * capacity, hid), F32),
+            pltpu.VMEM((2, 2 * capacity, 128), F32),
             pltpu.VMEM((2 * capacity, hid), BF16),
-            pltpu.VMEM((2 * capacity, 128), F32),
+            pltpu.VMEM((2, 2 * capacity, 128), F32),
             pltpu.VMEM((2, 2, n_tok, 128), F32),
             pltpu.VMEM((4, n_tok, 128), F32),
             pltpu.VMEM((2, 2, 2, n_tok, feat), BF16),
@@ -559,26 +543,21 @@
             pltpu.VMEM((2,) + half, BF16),
             pltpu.VMEM(half, BF16),
             pltpu.VMEM(half, BF16),
-            pltpu.VMEM((n_tok, feat), BF16),
-            pltpu.VMEM(kv_shape, F32),
-            pltpu.VMEM(kv_shape, F32),
-            pltpu.VMEM(kv_shape, F32),
-            pltpu.VMEM((2, 2) + part, BF16),
-            pltpu.VMEM((2,) + part, BF16),
-            pltpu.VMEM(part, BF16),
-            pltpu.VMEM((2, 2) + part, BF16),
-            pltpu.SemaphoreType.DMA((36,)),
-            pltpu.SemaphoreType.DMA((36,)),
-            pltpu.SemaphoreType.DMA((9,)),
-            pltpu.SemaphoreType.DMA((10,)),
+            pltpu.VMEM((4,) + part, F32),
+            pltpu.VMEM((4,) + part, BF16),
+            pltpu.VMEM((3,) + part, BF16),
+            pltpu.VMEM((4,) + part, BF16),
+            pltpu.SemaphoreType.DMA((38,)),
+            pltpu.SemaphoreType.DMA((38,)),
+            pltpu.SemaphoreType.DMA((11,)),
         ],
         compiler_params=pltpu.CompilerParams(
-            collective_id=0, has_side_effects=True, vmem_limit_bytes=56 << 20
+            collective_id=0, has_side_effects=True, vmem_limit_bytes=48 << 20
         ),
         name="step",
     )(
         tokens,
-        ids,
+        expert_ids,
         router,
         router_moment,
         router_grads,
@@ -589,6 +568,7 @@
         w_up,
         w_down,
     )
+    return held
 
 
 def solution(mesh):

time: 74.1 us -> 72 us (0.972)
  the two profiles are of different devices: /device:TPU:0 before, /device:TPU:9 now
where the time goes in v2:
time: 72 us; the launch traced here: 71.6 us
  Pallas kernels  62.3 us (87%)
  local copies, waits for them, and re-layouts  8.62 us (12%)
    pallas_call x1, Pallas kernels, fused(): pl.pallas_call(functools.partial(kernel, capacity), out_shape=tuple((pltp...  62.3 us
    unnamed x14, local copies, waits for them, and re-layouts  8.62 us

profile of v2, /device:TPU:9, one launch (start us, length us, event | category | flops | bytes accessed | tf_op | source)
XLA Modules:
  0.0 71.6 jit_solution(17206755118352297868)
XLA Ops:
  0.6 0.8 %copy.16.ids = s32[128,2]{1,0:T(8,128)S(1)} copy(s32[128,2]{0,1:T(2,128)} %param.12) | data formatting | bytes 2048 | tf_op args[1]
  1.4 0.0 copy-start
  1.4 1.0 %copy-done = bf16[128,2048]{1,0:T(8,128)(2,1)S(1)} copy-done((bf16[128,2048]{1,0:T(8,128)(2,1)S(1)}, bf16[128,2048]{1,0:T(8,128)(2,1)}, u32[]{:S(2)}) %copy-start) | copy-done | bytes 524312
  2.5 0.0 copy-start.1
  2.5 0.7 copy-done.1
  3.2 0.0 copy-start.2
  3.2 0.7 copy-done.2
  3.9 0.0 copy-start.3
  3.9 0.7 copy-done.3
  4.6 62.3 %step.1 = (bf16[128,2048]{1,0:T(8,128)(2,1)S(1)}, f32[1,4096]{1,0:T(1,128)S(1)}, f32[1,4096]{1,0:T(1,128)S(1)}, f32[1024,512]{1,0:T(8,128)S(1)}, f32[1024,512]{1,0:T(8,128)S(1)}) custom-call(bf16[128,2048]{1,0:T(8,128)(2,1)S(1)} %copy-done, s32[128,2]{1,0:T(8,128)S(1)} %copy.16.ids, f32[1,4096]{1,0:T(1,128)S(1)} %copy-done.1, f32[1,4096]{1,0:T(1,128)S(1)} %copy-done.2, ...), custom_call_target="tpu_custom_call" | custom-call | tf_op jit(solution)/shard_map/step/pallas_call | solution.py:520
  66.9 0.8 %copy.22 = bf16[128,2048]{1,0:T(8,128)(2,1)} copy(bf16[128,2048]{1,0:T(8,128)(2,1)S(1)} %get-tuple-element.5) | data formatting | bytes 1048576
  67.7 0.6 copy.23
  68.3 0.6 copy.24
  68.9 1.3 %copy.25 = f32[1024,512]{1,0:T(8,128)} copy(f32[1024,512]{1,0:T(8,128)S(1)} %get-tuple-element.8) | data formatting | bytes 4194304
  70.2 1.3 %copy.26 = f32[1024,512]{1,0:T(8,128)} copy(f32[1024,512]{1,0:T(8,128)S(1)} %get-tuple-element.9) | data formatting | bytes 4194304
Async XLA Ops:
  1.4 1.0 %copy-start = (bf16[128,2048]{1,0:T(8,128)(2,1)S(1)}, bf16[128,2048]{1,0:T(8,128)(2,1)}, u32[]{:S(2)}) copy-start(bf16[128,2048]{1,0:T(8,128)(2,1)} %tokens.1) | copy-start | bytes 1572868
  2.5 0.7 %copy-start.1 = (f32[1,4096]{1,0:T(1,128)S(1)}, f32[1,4096]{1,0:T(1,128)}, u32[]{:S(2)}) copy-start(f32[1,4096]{1,0:T(1,128)} %router.1) | copy-start | bytes 49156
  3.2 0.7 %copy-start.2 = (f32[1,4096]{1,0:T(1,128)S(1)}, f32[1,4096]{1,0:T(1,128)}, u32[]{:S(2)}) copy-start(f32[1,4096]{1,0:T(1,128)} %router_moment.1) | copy-start | bytes 49156
  3.9 0.7 %copy-start.3 = (f32[1,1,4096]{2,1,0:T(1,128)S(1)}, f32[1,1,4096]{2,1,0:T(1,128)}, u32[]{:S(2)}) copy-start(f32[1,1,4096]{2,1,0:T(1,128)} %router_grads.1) | copy-start | bytes 49156

commit v3 on v2

--- a/solution.py
+++ b/solution.py
@@ -422,6 +422,7 @@
     expert_rows(1, 1)
     expert_out(0, 0)
     send(outp.at[0, 0, 0], sib.at[0, 0], 25, sibling)
+    sum_quarter()
     expert_hidden(1)
     expert_out(1, 1)
     send(outp.at[1, 0, 1], sib.at[1, 1], 28, sibling)
@@ -434,8 +435,6 @@
     arrive(sib.at[1, 0], 29, sibling)
     add_rows(outp.at[1, 1, 0], outp.at[1, 1, 0], sib.at[1, 0], 0, n_tok)
     send(outp.at[1, 1, 0, B], yb.at[0], 32, yn)
-
-    sum_quarter()
 
     arrive(sib.at[0, 0], 25, sibling)
     add_rows(outp.at[0, 1, 0], outp.at[0, 1, 0], sib.at[0, 0], 0, n_tok)
@@ -552,7 +551,7 @@
             pltpu.SemaphoreType.DMA((11,)),
         ],
         compiler_params=pltpu.CompilerParams(
-            collective_id=0, has_side_effects=True, vmem_limit_bytes=48 << 20
+            collective_id=0, has_side_effects=True, vmem_limit_bytes=59 << 20
         ),
         name="step",
     )(

time: 72 us -> 67.2 us (0.933)
  the two profiles are of different devices: /device:TPU:9 before, /device:TPU:0 now
where the time goes in v3:
time: 67.2 us; the launch traced here: 66.9 us
  Pallas kernels  60.3 us (90%)
  local copies, waits for them, and re-layouts  6.06 us (9%)
    pallas_call x1, Pallas kernels, fused(): pl.pallas_call(functools.partial(kernel, capacity), out_shape=tuple((pltp...  60.3 us
    unnamed x6, local copies, waits for them, and re-layouts  6.06 us

profile of v3, /device:TPU:0, one launch (start us, length us, event | category | flops | bytes accessed | tf_op | source)
XLA Modules:
  0.0 66.9 jit_solution(8701578935572812317)
XLA Ops:
  0.6 1.4 %copy.16.ids = s32[128,2]{1,0:T(8,128)} copy(s32[128,2]{0,1:T(2,128)} %param.12) | data formatting | bytes 2048 | tf_op args[1]
  2.0 60.3 %step.1 = (bf16[128,2048]{1,0:T(8,128)(2,1)S(1)}, f32[1,4096]{1,0:T(1,128)S(1)}, f32[1,4096]{1,0:T(1,128)S(1)}, f32[1024,512]{1,0:T(8,128)S(1)}, f32[1024,512]{1,0:T(8,128)S(1)}) custom-call(bf16[128,2048]{1,0:T(8,128)(2,1)} %tokens.1, s32[128,2]{1,0:T(8,128)} %copy.16.ids, f32[1,4096]{1,0:T(1,128)} %router.1, f32[1,4096]{1,0:T(1,128)} %router_moment.1, ...), custom_call_target="tpu_custom_call" | custom-call | tf_op jit(solution)/shard_map/step/pallas_call | solution.py:519
  62.3 0.8 %copy.22 = bf16[128,2048]{1,0:T(8,128)(2,1)} copy(bf16[128,2048]{1,0:T(8,128)(2,1)S(1)} %get-tuple-element.5) | data formatting | bytes 1048576
  63.1 0.6 copy.23
  63.7 0.6 copy.24
  64.3 1.3 %copy.25 = f32[1024,512]{1,0:T(8,128)} copy(f32[1024,512]{1,0:T(8,128)S(1)} %get-tuple-element.8) | data formatting | bytes 4194304
  65.6 1.3 %copy.26 = f32[1024,512]{1,0:T(8,128)} copy(f32[1024,512]{1,0:T(8,128)S(1)} %get-tuple-element.9) | data formatting | bytes 4194304
